TPU v7x, 32 devices: a whole 2x2x4 slice. The times are simulated.
32 devices in a mesh: row: 8 (over y, x, core), col: 4 (over z).
Axes of the slice: x: 2, y: 2, z: 4, core: 2. Of those that a mesh axis runs over, the one named last changes fastest.
Arguments:
- covariance: float32 [8192, 8192], P('row', 'col'), as said below
- innovations: float32 [512, 8, 1024], P('row', None, 'col'), may hold values from -6 to 6
- block_owner: int32 [32], replicated, may hold values from 0 to 31, as said below
- panel_index: int32 [1], replicated, may hold values from 0 to 15
Outputs:
- factor: float32 [8192, 8192], P('row', 'col')
- solved: float32 [512, 8192], P('col', 'row')
Inputs may be any that keep to these rules, and one draw needn't show every extreme that they name: Storage block s holds global block block_owner[s]; every global block appears once; the storage blocks s with one value of s // 4 hold the blocks of one residue modulo 8, rising with s. `covariance`: symmetric positive definite.
All inputs are finite; a program needn't handle non-finite values.
Results may differ from a plain program's by a relative error of at most 0.0016.
Values may be sent and summed in bfloat16 or wider, within the bound.
A program may use at most 128 MiB of HBM per device.

v0:
```python
import jax
import jax.numpy as jnp
from jax import lax
from jax.sharding import PartitionSpec as P

B = 256
PANELS = 2
CONTRACT_LAST = (((1,), (1,)), ((), ()))


def spread(value, axis, source):
    kept = jnp.where(lax.axis_index(axis) == source, value, 0).astype(value.dtype)
    return lax.psum(kept, axis)


def lower_solve(factor, right_side):
    return jax.scipy.linalg.solve_triangular(factor, right_side, lower=True)


def outer_rows(left, right):
    return lax.dot_general(left, right, CONTRACT_LAST, preferred_element_type=jnp.float32)


def locate(block_owner, target):
    positions = jnp.arange(block_owner.shape[0], dtype=jnp.int32)
    return jnp.sum(jnp.where(block_owner == target, positions, 0))


def per_device(covariance, innovations, block_owner, panel_index):
    panel_width = B
    local_rows, local_cols = covariance.shape
    row_blocks = local_rows // panel_width
    column_blocks = local_cols // panel_width
    row_here = lax.axis_index("row")
    column_here = lax.axis_index("col")
    relaid = lax.all_to_all(
        lax.all_to_all(innovations, "row", split_axis=1, concat_axis=0, tiled=True),
        "col",
        split_axis=0,
        concat_axis=2,
        tiled=True,
    )
    solved = relaid.reshape(relaid.shape[0], local_rows)
    owner_rows = jnp.repeat(
        lax.dynamic_slice_in_dim(block_owner, row_here * row_blocks, row_blocks), panel_width
    )
    owner_columns = jnp.repeat(
        lax.dynamic_slice_in_dim(block_owner, column_here * column_blocks, column_blocks),
        panel_width,
    )
    matrix = covariance
    ahead_column = None
    for panel_turn in range(PANELS):
        target = panel_index[0] + panel_turn
        slot_index = locate(block_owner, target)
        row_root = slot_index // row_blocks
        column_root = slot_index // column_blocks
        row_start = slot_index % row_blocks * panel_width
        column_start = slot_index % column_blocks * panel_width
        column_local = lax.dynamic_slice_in_dim(matrix, column_start, panel_width, 1)
        ahead_column = None
        live_rows = owner_rows > target
        live_columns = owner_columns > target
        column = spread(column_local, "col", column_root)
        diagonal_local = lax.dynamic_slice_in_dim(column, row_start, panel_width, 0)
        innovation_local = lax.dynamic_slice_in_dim(solved, row_start, panel_width, 1)
        diagonal, innovation_block = (
            spread(diagonal_local, "row", row_root),
            spread(innovation_local, "row", row_root),
        )
        factor = jnp.linalg.cholesky(diagonal)
        panel_rows = jnp.where(live_rows[:, None], lower_solve(factor, column.T).T, 0.0)
        rows_half = panel_rows.astype(jnp.bfloat16)
        row_local = lax.dynamic_slice_in_dim(matrix, row_start, panel_width, 0)
        row_panel = spread(row_local, "row", row_root)
        panel_columns = jnp.where(live_columns[:, None], lower_solve(factor, row_panel).T, 0.0)
        columns_half = panel_columns.astype(jnp.bfloat16)
        matrix = matrix - outer_rows(rows_half, columns_half)
        whitened = lower_solve(factor, innovation_block.T).T
        solved = solved - outer_rows(whitened.astype(jnp.bfloat16), rows_half)
        spot_old = lax.dynamic_slice_in_dim(solved, row_start, panel_width, 1)
        spot_new = jnp.where(row_here == row_root, whitened, spot_old)
        solved = lax.dynamic_update_slice_in_dim(solved, spot_new, row_start, 1)
        row_old = lax.dynamic_slice_in_dim(matrix, row_start, panel_width, 0)
        row_new = jnp.where((row_here == row_root) & live_columns[None, :], 0.0, row_old)
        matrix = lax.dynamic_update_slice_in_dim(matrix, row_new, row_start, 0)
        column_old = lax.dynamic_slice_in_dim(matrix, column_start, panel_width, 1)
        column_new = jnp.where(live_rows[:, None], panel_rows, column_old)
        diagonal_spot = lax.dynamic_update_slice_in_dim(column_new, factor, row_start, 0)
        column_new = jnp.where(row_here == row_root, diagonal_spot, column_new)
        column_new = jnp.where(column_here == column_root, column_new, column_old)
        matrix = lax.dynamic_update_slice_in_dim(matrix, column_new, column_start, 1)
    return (matrix, solved)


def solution(mesh):
    placed = (P("row", "col"), P("row", None, "col"), P(), P())
    return jax.shard_map(
        per_device,
        mesh=mesh,
        in_specs=placed,
        out_specs=(P("row", "col"), P("col", "row")),
        check_vma=False,
    )
```

profile of v0, /device:TPU:0, one launch (start us, length us, event | category | flops | bytes accessed | tf_op | source)
XLA Modules:
  0.0 469.5 jit_solution(13405228891102686264)
XLA Ops:
  7.2 2.0 copy.81
  9.2 5.2 %all-to-all-start = ((f32[64,8,256]{2,0,1:T(8,128)}), f32[64,8,256]{2,0,1:T(8,128)S(1)}, u32[]{:S(2)}, u32[]{:S(2)}) async-start(f32[64,8,256]{2,0,1:T(8,128)} %copy.81), calls=%async_computation | async-start | bytes 1048576 | tf_op jit(solution)/shard_map/all_to_all | solution.py:37
  18.3 9.3 %copy.69 = f32[1024,2048]{0,1:T(8,128)} copy(f32[1024,2048]{1,0:T(8,128)} %param.11) | data formatting | bytes 16777216 | tf_op args[0]
  27.6 2.3 dynamic-slice_select_fusion.3
  31.3 4.9 %all-to-all-start.1 = ((f32[512,1,256]{2,1,0:T(1,128)}), f32[512,1,256]{2,1,0:T(1,128)S(1)}, u32[]{:S(2)}, u32[]{:S(2)}) async-start(f32[512,1,256]{2,1,0:T(1,128)} %copy.82), calls=%async_computation.1 | async-start | bytes 1048576 | tf_op jit(solution)/shard_map/all_to_all | solution.py:36
  36.2 3.2 dynamic-slice_select_fusion.1
  39.4 55.2 %all-reduce.8.cloned.1.call-done = f32[1024,256]{0,1:T(8,128)} async-done(((f32[1024,256]{0,1:T(8,128)}), f32[1024,256]{0,1:T(8,128)}) %all-reduce.8.cloned.1.call-update) | async-done | bytes 1048592 | tf_op jit(solution)/shard_map/psum | solution.py:13
  100.2 61.6 %all-reduce.14.cloned.1.call-done = (f32[256,2048]{0,1:T(8,128)}, f32[256,256]{0,1:T(8,128)}, f32[256,128]{1,0:T(8,128)}) async-done(((f32[256,2048]{0,1:T(8,128)}, f32[256,256]{0,1:T(8,128)}, f32[256,128]{1,0:T(8,128)}), (f32[256,2048]{0,1:T(8,128)}, f32[256,256]{0,1:T(8,128)}, f32[256,128]{1,0:T(8,128)})) %all-reduce.14.cloned.1.call-update) | async-done | bytes 2490384 | tf_op jit(solution)/shard_map/psum | solution.py:13
  163.9 11.7 %cholesky.130 = f32[128,128]{1,0:T(8,128)S(1)} custom-call(f32[128,128]{1,0:T(8,128)S(1)} %cholesky.194), custom_call_target="Cholesky" | custom-call | tf_op jit(solution)/shard_map/jit(cholesky)/cholesky | solution.py:71
  175.6 9.8 %custom-call.21 = f32[1,128,128]{1,2,0:T(8,128)S(1)} custom-call(f32[1,128,128]{2,1,0:T(8,128)S(1)} %get-tuple-element.163), custom_call_target="InvertDiagBlocksLowerTriangular" | custom-call | tf_op jit(solution)/shard_map/jit(cholesky)/cholesky | solution.py:71
  185.9 11.7 %cholesky.147 = f32[128,128]{1,0:T(8,128)S(1)} custom-call(f32[128,128]{1,0:T(8,128)S(1)} %convolution_subtract_fusion.11), custom_call_target="Cholesky" | custom-call | tf_op jit(solution)/shard_map/jit(cholesky)/cholesky | solution.py:71
  200.1 4.6 while.12
  204.7 19.7 %custom-call.22 = f32[2,128,128]{1,2,0:T(8,128)S(1)} custom-call(f32[2,128,128]{2,1,0:T(8,128)S(1)} %get-tuple-element.48), custom_call_target="InvertDiagBlocksLowerTriangular" | custom-call | tf_op jit(solution)/shard_map/jit(_solve_triangular)/triangular_solve | solution.py:17
  224.4 2.3 fusion.6
  226.7 3.1 convolution_subtract_fusion.3
  232.7 1.7 convolution_subtract_fusion.7
  236.1 4.3 convolution_subtract_fusion.1
  241.4 3.4 copy-done
  247.8 3.0 dynamic-slice_select_fusion
  250.8 46.6 %all-reduce.10.cloned.1.call-done = f32[1024,256]{0,1:T(8,128)} async-done(((f32[1024,256]{0,1:T(8,128)}), f32[1024,256]{0,1:T(8,128)}) %all-reduce.10.cloned.1.call-update) | async-done | bytes 1048592 | tf_op jit(solution)/shard_map/psum | solution.py:13
  299.3 65.3 %all-reduce.12.cloned.1.call-done = (f32[256,2048]{0,1:T(8,128)}, f32[256,256]{0,1:T(8,128)}, f32[256,128]{1,0:T(8,128)}) async-done(((f32[256,2048]{0,1:T(8,128)}, f32[256,256]{0,1:T(8,128)}, f32[256,128]{1,0:T(8,128)}), (f32[256,2048]{0,1:T(8,128)}, f32[256,256]{0,1:T(8,128)}, f32[256,128]{1,0:T(8,128)})) %all-reduce.12.cloned.1.call-update) | async-done | bytes 2490384 | tf_op jit(solution)/shard_map/psum | solution.py:13
  366.7 11.7 %cholesky.164 = f32[128,128]{1,0:T(8,128)S(1)} custom-call(f32[128,128]{1,0:T(8,128)S(1)} %cholesky.197), custom_call_target="Cholesky" | custom-call | tf_op jit(solution)/shard_map/jit(cholesky)/cholesky | solution.py:71
  378.4 9.8 %custom-call.24 = f32[1,128,128]{1,2,0:T(8,128)S(1)} custom-call(f32[1,128,128]{2,1,0:T(8,128)S(1)} %get-tuple-element.161), custom_call_target="InvertDiagBlocksLowerTriangular" | custom-call | tf_op jit(solution)/shard_map/jit(cholesky)/cholesky | solution.py:71
  388.7 11.7 %cholesky.181 = f32[128,128]{1,0:T(8,128)S(1)} custom-call(f32[128,128]{1,0:T(8,128)S(1)} %convolution_subtract_fusion.10), custom_call_target="Cholesky" | custom-call | tf_op jit(solution)/shard_map/jit(cholesky)/cholesky | solution.py:71
  403.5 4.4 while.13
  407.9 19.7 %custom-call.25 = f32[2,128,128]{1,2,0:T(8,128)S(1)} custom-call(f32[2,128,128]{2,1,0:T(8,128)S(1)} %get-tuple-element.50), custom_call_target="InvertDiagBlocksLowerTriangular" | custom-call | tf_op jit(solution)/shard_map/jit(_solve_triangular)/triangular_solve | solution.py:17
  427.6 2.3 fusion.4
  429.9 3.1 convolution_subtract_fusion.2
  440.2 6.2 %convolution_subtract_fusion = f32[1024,2048]{0,1:T(8,128)} fusion(f32[1024,2048]{0,1:T(8,128)} %copy-done, bf16[128,2048]{0,1:T(8,128)(2,1)S(1)} %fusion.43, bf16[128,2048]{0,1:T(8,128)(2,1)S(1)} %copy-done.1, pred[2048]{0:T(1024)(128)(4,1)S(1)} %gt.75, f32[128,1024]{1,0:T(8,128)S(1)} %fusion.44, f32[128,1024]{1,0:T(8,128)S(1)} %fusion.16, ...), kind=kOutput, calls=%fused_computation.4 | convolution fusion | flops 1079771136 | bytes 18877440 | tf_op jit(solution)/shard_map/dot_general | solution.py:21
  446.4 3.3 select_dynamic-update-slice_fusion
  451.2 2.4 select_dynamic-update-slice_fusion.2
  453.6 9.1 %copy.88 = f32[1024,2048]{1,0:T(8,128)} copy(f32[1024,2048]{0,1:T(8,128)} %select_dynamic-update-slice_fusion.2) | data formatting | bytes 16777216
  (125 shorter events, 40.4 us)
Async XLA Ops:
  7.2 7.9 %copy-start.6 = (s32[32]{0:T(128)S(1)}, s32[32]{0:T(128)}, u32[]{:S(2)}) copy-start(s32[32]{0:T(128)} %param.13) | copy-start | bytes 388
  9.2 20.8 %all-to-all-start = ((f32[64,8,256]{2,0,1:T(8,128)}), f32[64,8,256]{2,0,1:T(8,128)S(1)}, u32[]{:S(2)}, u32[]{:S(2)}) async-start(f32[64,8,256]{2,0,1:T(8,128)} %copy.81), calls=%async_computation | async-start | bytes 1048576 | tf_op jit(solution)/shard_map/all_to_all | solution.py:37
  14.4 80.1 %all-reduce.8.cloned.1.call-start = ((), (), s32[]{:S(2)}) async-start(), calls=%async_computation.2 | async-start | bytes 2097152 | tf_op jit(solution)/shard_map/psum | solution.py:13
  31.3 64.9 %all-to-all-start.1 = ((f32[512,1,256]{2,1,0:T(1,128)}), f32[512,1,256]{2,1,0:T(1,128)S(1)}, u32[]{:S(2)}, u32[]{:S(2)}) async-start(f32[512,1,256]{2,1,0:T(1,128)} %copy.82), calls=%async_computation.1 | async-start | bytes 1048576 | tf_op jit(solution)/shard_map/all_to_all | solution.py:36
  36.2 125.6 %all-reduce.14.cloned.1.call-start = ((), (), s32[]{:S(2)}) async-start(), calls=%async_computation.5 | async-start | bytes 4980736 | tf_op jit(solution)/shard_map/psum | solution.py:13
  97.1 200.3 %all-reduce.10.cloned.1.call-start = ((), (), s32[]{:S(2)}) async-start(), calls=%async_computation.3 | async-start | bytes 2097152 | tf_op jit(solution)/shard_map/psum | solution.py:13
  226.6 4.1 copy-start.4
  232.7 3.4 copy-start.2
  241.4 3.4 copy-start
  245.9 118.6 %all-reduce.12.cloned.1.call-start = ((), (), s32[]{:S(2)}) async-start(), calls=%async_computation.4 | async-start | bytes 4980736 | tf_op jit(solution)/shard_map/psum | solution.py:13
  429.9 4.1 copy-start.5
  434.0 2.6 copy-start.3
  438.2 2.0 copy-start.1
Sparse Core Ops, SparseCore 0:
  30.1 64.3 all-reduce.7
  98.6 63.1 all-reduce.13
  246.1 51.2 all-reduce.9
  301.4 63.1 all-reduce.11
where the time goes:
time: 473 us; the launch traced here: 469 us
  waiting for transfers between devices  229 us (48%)
  other arithmetic  133 us (28%)
  local copies, waits for them, and re-layouts  39.7 us (8%)
  matrix products  33.4 us (7%)
  between operations  22.7 us (5%)
  starting transfers between devices  10.7 us (2%)
    psum x4, waiting for transfers between devices, spread(): return lax.psum(kept, axis)  229 us
    another operation x13, other arithmetic, per_device(): factor = jnp.linalg.cholesky(diagonal)  68.6 us
    another operation x5, other arithmetic, lower_solve(): return jax.scipy.linalg.solve_triangular(factor, right_side, lower=True)  39.4 us
    unnamed x19, local copies, waits for them, and re-layouts  24.8 us
    another operation x18, matrix products, lower_solve(): return jax.scipy.linalg.solve_triangular(factor, right_side, lower=True)  21.3 us
    select_n x6, other arithmetic, spread(): jnp.where(lax.axis_index(axis) == source, value, 0).astype(value.dtype)  13 us
    dot_general x4, matrix products, outer_rows(): lax.dot_general(left, right, CONTRACT_LAST, preferred_element_type=jnp.fl...  11.2 us
    another operation x25, local copies, waits for them, and re-layouts, lower_solve(): return jax.scipy.linalg.solve_triangular(factor, right_side, lower=True)  10.2 us
  transfers between devices with their start and end apart: 6, of which 4 were waited for; matrix products, arithmetic and copies ran while one was open for 5% of the time, Pallas kernels for 0%

commit v1 on v0

--- a/solution.py
+++ b/solution.py
@@ -8,9 +8,15 @@
 CONTRACT_LAST = (((1,), (1,)), ((), ()))
 
 
+def add_all(block, axis):
+    parts = lax.all_gather(block, axis, axis=0, tiled=False)
+    acc = parts.sum(axis=0)
+    return acc
+
+
 def spread(value, axis, source):
     kept = jnp.where(lax.axis_index(axis) == source, value, 0).astype(value.dtype)
-    return lax.psum(kept, axis)
+    return add_all(kept, axis)
 
 
 def lower_solve(factor, right_side):

time: 473 us -> 509 us (1.076)
  waiting for transfers between devices: 229 us -> 266 us
  other arithmetic: 133 us -> 150 us
  local copies, waits for them, and re-layouts: 39.7 us -> 23.6 us
  blocking collectives: 0 us -> 13.6 us
  matrix products: 33.4 us -> 23.3 us
  starting transfers between devices: 10.7 us -> 5.33 us
    all_gather x0 -> x8, waiting for transfers between devices: none -> 256 us  [add_all(): parts = lax.all_gather(block, axis, axis=0, tiled=False)]
    psum x4 -> x0, waiting for transfers between devices: 229 us -> none  [spread(): return lax.psum(kept, axis)]
    reduce_sum x0 -> x8, other arithmetic: none -> 24.7 us  [add_all(): acc = parts.sum(axis=0)]
    all_to_all x0 -> x1, blocking collectives: none -> 13.6 us  [per_device(): lax.all_to_all(innovations, 'row', split_axis=1, concat_axis=0, tiled=True)]
    unnamed x19 -> x31, local copies, waits for them, and re-layouts: 24.8 us -> 13.4 us
    all_to_all x1, waiting for transfers between devices: 0.01 us -> 9.94 us  [per_device(): lax.all_to_all(lax.all_to_all(innovations, 'row', split_axis=1, concat_ax...]
    another operation x18, matrix products: 21.3 us -> 12.3 us  [lower_solve(): return jax.scipy.linalg.solve_triangular(factor, right_side, lower=True)]
    all_to_all x1 -> x0, starting transfers between devices: 5.2 us -> none  [per_device(): lax.all_to_all(innovations, 'row', split_axis=1, concat_axis=0, tiled=True)]
  transfers between devices with their start and end apart: 6 -> 9, of which waited for: 4 -> 8; matrix products, arithmetic and copies ran while one was open for 5% -> 32% of each run, Pallas kernels for 0% -> 0%
where the time goes in v1:
time: 509 us; the launch traced here: 506 us
  waiting for transfers between devices  266 us (52%)
  other arithmetic  150 us (29%)
  local copies, waits for them, and re-layouts  23.6 us (5%)
  matrix products  23.3 us (5%)
  between operations  23.2 us (5%)
  blocking collectives  13.6 us (3%)
  starting transfers between devices  5.33 us (1%)
    all_gather x8, waiting for transfers between devices, add_all(): parts = lax.all_gather(block, axis, axis=0, tiled=False)  256 us
    another operation x13, other arithmetic, per_device(): factor = jnp.linalg.cholesky(diagonal)  68.5 us
    another operation x5, other arithmetic, lower_solve(): return jax.scipy.linalg.solve_triangular(factor, right_side, lower=True)  39.4 us
    reduce_sum x8, other arithmetic, add_all(): acc = parts.sum(axis=0)  24.7 us
    all_to_all x1, blocking collectives, per_device(): lax.all_to_all(innovations, 'row', split_axis=1, concat_axis=0, tiled=True)  13.6 us
    unnamed x31, local copies, waits for them, and re-layouts  13.4 us
    select_n x8, other arithmetic, spread(): jnp.where(lax.axis_index(axis) == source, value, 0).astype(value.dtype)  12.5 us
    another operation x18, matrix products, lower_solve(): return jax.scipy.linalg.solve_triangular(factor, right_side, lower=True)  12.3 us
  transfers between devices with their start and end apart: 9, of which 8 were waited for; matrix products, arithmetic and copies ran while one was open for 32% of the time, Pallas kernels for 0%

profile of v1, /device:TPU:0, one launch (start us, length us, event | category | flops | bytes accessed | tf_op | source)
XLA Modules:
  0.0 505.9 jit_solution(16445608573165710677)
XLA Ops:
  11.8 2.3 dynamic-slice_select_fusion.3
  14.2 83.5 %all-gather.17.cloned.1.call-done = f32[4096,256]{1,0:T(8,128)} async-done(((f32[1024,256]{1,0:T(8,128)}), f32[4096,256]{1,0:T(8,128)}) %all-gather.17.cloned.1.call-update) | async-done | bytes 4194320 | tf_op jit(solution)/shard_map/all_gather | solution.py:12
  97.7 2.6 reduce_sum.91
  101.1 3.1 dynamic-slice_select_fusion.1
  105.5 13.6 %all_to_all.33 = f32[64,8,256]{2,0,1:T(8,128)S(1)} all-to-all(f32[64,8,256]{2,0,1:T(8,128)S(1)} %copy.34), channel_id=1, replica_groups=mesh['row'=8,'col'=4] {'row'}, dimensions={1} | all-to-all | bytes 1048576 | tf_op jit(solution)/shard_map/all_to_all | solution.py:43
  120.4 4.4 all-to-all-start.1
  128.3 9.9 %all-to-all-done.1 = f32[512,1,256]{2,1,0:T(1,128)S(1)} async-done(((f32[512,1,256]{2,1,0:T(1,128)}), f32[512,1,256]{2,1,0:T(1,128)S(1)}, u32[]{:S(2)}, u32[]{:S(2)}) %all-to-all-start.1) | async-done | bytes 524320 | tf_op jit(solution)/shard_map/all_to_all | solution.py:42
  139.4 1.8 reduce_sum.92
  141.4 11.7 %cholesky.130 = f32[128,128]{1,0:T(8,128)S(1)} custom-call(f32[128,128]{1,0:T(8,128)S(1)} %cholesky.194), custom_call_target="Cholesky" | custom-call | tf_op jit(solution)/shard_map/jit(cholesky)/cholesky | solution.py:77
  153.2 9.8 %custom-call.21 = f32[1,128,128]{1,2,0:T(8,128)S(1)} custom-call(f32[1,128,128]{2,1,0:T(8,128)S(1)} %get-tuple-element.89), custom_call_target="InvertDiagBlocksLowerTriangular" | custom-call | tf_op jit(solution)/shard_map/jit(cholesky)/cholesky | solution.py:77
  163.5 11.7 %cholesky.147 = f32[128,128]{1,0:T(8,128)S(1)} custom-call(f32[128,128]{1,0:T(8,128)S(1)} %convolution_subtract_fusion.11), custom_call_target="Cholesky" | custom-call | tf_op jit(solution)/shard_map/jit(cholesky)/cholesky | solution.py:77
  177.2 4.0 while.12
  181.7 19.7 %custom-call.22 = f32[2,128,128]{1,2,0:T(8,128)S(1)} custom-call(f32[2,128,128]{2,1,0:T(8,128)S(1)} %get-tuple-element.48), custom_call_target="InvertDiagBlocksLowerTriangular" | custom-call | tf_op jit(solution)/shard_map/jit(_solve_triangular)/triangular_solve | solution.py:23
  203.8 21.3 %all-gather.21.cloned.1.call-done = f32[2048,2048]{1,0:T(8,128)} async-done(((f32[256,2048]{1,0:T(8,128)}), f32[2048,2048]{1,0:T(8,128)}) %all-gather.21.cloned.1.call-update) | async-done | bytes 16777232 | tf_op jit(solution)/shard_map/all_gather | solution.py:12
  225.1 7.8 %reduce_sum.93 = f32[256,2048]{1,0:T(8,128)S(1)} reduce(f32[8,256,2048]{2,1,0:T(8,128)} %bitcast.162, f32[]{:T(128)} %constant.160.clone.1), dimensions={0}, to_apply=%region_7.10 | reduce | flops 3670016 | bytes 18874372 | tf_op jit(solution)/shard_map/reduce_sum | solution.py:13
  236.1 4.7 convolution_subtract_fusion.1
  242.3 3.4 copy-done
  247.4 3.0 all-gather.29.cloned.1.call-done
  254.0 78.6 %all-gather.23.cloned.1.call-done = f32[4096,256]{1,0:T(8,128)} async-done(((f32[1024,256]{1,0:T(8,128)}), f32[4096,256]{1,0:T(8,128)}) %all-gather.23.cloned.1.call-update) | async-done | bytes 4194320 | tf_op jit(solution)/shard_map/all_gather | solution.py:12
  332.5 2.6 reduce_sum.95
  335.9 3.2 dynamic-slice_select_fusion
  339.9 16.4 %all-gather.31.cloned.1.call-done = f32[1024,256]{0,1:T(8,128)} async-done(((f32[128,256]{0,1:T(8,128)}), f32[1024,256]{0,1:T(8,128)}) %all-gather.31.cloned.1.call-update) | async-done | bytes 1048592 | tf_op jit(solution)/shard_map/all_gather | solution.py:12
  358.0 28.6 %all-gather.25.cloned.1.call-done = f32[2048,256]{1,0:T(8,128)} async-done(((f32[256,256]{1,0:T(8,128)}), f32[2048,256]{1,0:T(8,128)}) %all-gather.25.cloned.1.call-update) | async-done | bytes 2097168 | tf_op jit(solution)/shard_map/all_gather | solution.py:12
  388.5 11.7 %cholesky.164 = f32[128,128]{1,0:T(8,128)S(1)} custom-call(f32[128,128]{1,0:T(8,128)S(1)} %cholesky.197), custom_call_target="Cholesky" | custom-call | tf_op jit(solution)/shard_map/jit(cholesky)/cholesky | solution.py:77
  400.3 9.8 %custom-call.24 = f32[1,128,128]{1,2,0:T(8,128)S(1)} custom-call(f32[1,128,128]{2,1,0:T(8,128)S(1)} %get-tuple-element.85), custom_call_target="InvertDiagBlocksLowerTriangular" | custom-call | tf_op jit(solution)/shard_map/jit(cholesky)/cholesky | solution.py:77
  410.6 11.7 %cholesky.181 = f32[128,128]{1,0:T(8,128)S(1)} custom-call(f32[128,128]{1,0:T(8,128)S(1)} %convolution_subtract_fusion.10), custom_call_target="Cholesky" | custom-call | tf_op jit(solution)/shard_map/jit(cholesky)/cholesky | solution.py:77
  425.0 4.2 while.13
  429.1 19.7 %custom-call.25 = f32[2,128,128]{1,2,0:T(8,128)S(1)} custom-call(f32[2,128,128]{2,1,0:T(8,128)S(1)} %get-tuple-element.50), custom_call_target="InvertDiagBlocksLowerTriangular" | custom-call | tf_op jit(solution)/shard_map/jit(_solve_triangular)/triangular_solve | solution.py:23
  453.4 24.8 %all-gather.27.cloned.1.call-done = f32[2048,2048]{1,0:T(8,128)} async-done(((f32[256,2048]{1,0:T(8,128)}), f32[2048,2048]{1,0:T(8,128)}) %all-gather.27.cloned.1.call-update) | async-done | bytes 16777232 | tf_op jit(solution)/shard_map/all_gather | solution.py:12
  478.3 7.8 %reduce_sum.97 = f32[256,2048]{1,0:T(8,128)S(1)} reduce(f32[8,256,2048]{2,1,0:T(8,128)} %bitcast.163, f32[]{:T(128)} %constant.160.clone.1), dimensions={0}, to_apply=%region_11.15 | reduce | flops 3670016 | bytes 18874372 | tf_op jit(solution)/shard_map/reduce_sum | solution.py:13
  489.2 4.7 convolution_subtract_fusion
  495.5 3.4 copy-done.1
  (138 shorter events, 45.1 us)
Async XLA Ops:
  7.2 90.5 %all-gather.17.cloned.1.call-start = ((), (), s32[]{:S(2)}) async-start(), calls=%async_computation.2 | async-start | bytes 5242880 | tf_op jit(solution)/shard_map/all_gather | solution.py:12
  14.1 125.3 %all-gather.19.cloned.1.call-start = ((), (), s32[]{:S(2)}) async-start(), calls=%async_computation.3 | async-start | bytes 2359296 | tf_op jit(solution)/shard_map/all_gather | solution.py:12
  101.1 124.0 %all-gather.21.cloned.1.call-start = ((), (), s32[]{:S(2)}) async-start(), calls=%async_computation.4 | async-start | bytes 18874368 | tf_op jit(solution)/shard_map/all_gather | solution.py:12
  104.2 1.0 copy-start.8
  105.3 22.0 %copy-start.9 = (s32[32]{0:T(128)S(1)}, s32[32]{0:T(128)}, u32[]{:S(2)}) copy-start(s32[32]{0:T(128)} %param.13) | copy-start | bytes 388
  120.4 17.8 %all-to-all-start.1 = ((f32[512,1,256]{2,1,0:T(1,128)}), f32[512,1,256]{2,1,0:T(1,128)S(1)}, u32[]{:S(2)}, u32[]{:S(2)}) async-start(f32[512,1,256]{2,1,0:T(1,128)} %copy.35), calls=%async_computation.1 | async-start | bytes 1048576 | tf_op jit(solution)/shard_map/all_to_all | solution.py:42
  124.8 125.5 %all-gather.29.cloned.1.call-start = ((), (), s32[]{:S(2)}) async-start(), calls=%async_computation.8 | async-start | bytes 1179648 | tf_op jit(solution)/shard_map/all_gather | solution.py:12
  138.4 3.0 copy-start.2
  139.2 193.4 %all-gather.23.cloned.1.call-start = ((), (), s32[]{:S(2)}) async-start(), calls=%async_computation.5 | async-start | bytes 5242880 | tf_op jit(solution)/shard_map/all_gather | solution.py:12
  175.2 26.2 %copy-start.6 = (f32[256,256]{1,0:T(8,128)}, f32[256,256]{1,0:T(8,128)S(1)}, u32[]{:S(2)}) copy-start(f32[256,256]{1,0:T(8,128)S(1)} %get-tuple-element.87) | copy-start | bytes 786436
  181.2 0.6 copy-start.11
  241.0 1.0 copy-start.7
  242.3 3.4 copy-start
  246.8 6.0 %copy-start.3 = (f32[128,1,4,256]{0,3,2,1:T(8,128)S(1)}, f32[128,1,4,256]{0,3,2,1:T(8,128)}, u32[]{:S(2)}) copy-start(f32[128,1,4,256]{0,3,2,1:T(8,128)} %copy-done.2) | copy-start | bytes 1572868
  246.9 109.4 %all-gather.31.cloned.1.call-start = ((), (), s32[]{:S(2)}) async-start(), calls=%async_computation.9 | async-start | bytes 1179648 | tf_op jit(solution)/shard_map/all_gather | solution.py:12
  253.9 132.6 %all-gather.25.cloned.1.call-start = ((), (), s32[]{:S(2)}) async-start(), calls=%async_computation.6 | async-start | bytes 2359296 | tf_op jit(solution)/shard_map/all_gather | solution.py:12
  335.9 142.4 %all-gather.27.cloned.1.call-start = ((), (), s32[]{:S(2)}) async-start(), calls=%async_computation.7 | async-start | bytes 18874368 | tf_op jit(solution)/shard_map/all_gather | solution.py:12
  339.1 0.7 copy-start.10
  388.3 36.6 %copy-start.12 = (s32[2,2]{1,0:T(2,128)S(1)}, s32[2,2]{1,0:T(2,128)}, u32[]{:S(2)}) copy-start(s32[2,2]{1,0:T(2,128)} %copy-done.11) | copy-start | bytes 52
  423.0 25.8 %copy-start.4 = (f32[256,256]{1,0:T(8,128)}, f32[256,256]{1,0:T(8,128)S(1)}, u32[]{:S(2)}) copy-start(f32[256,256]{1,0:T(8,128)S(1)} %get-tuple-element.83) | copy-start | bytes 786436
  494.2 1.0 copy-start.5
  495.5 3.4 copy-start.1
Sparse Core Ops, SparseCore 0:
  14.2 83.4 all-gather.16
  101.2 31.5 all-gather.18
  135.2 89.8 all-gather.20
  226.8 23.4 all-gather.28
  251.8 80.7 all-gather.22
  334.3 21.9 all-gather.30
  358.7 27.7 all-gather.24
  388.4 89.7 all-gather.26
